TPU v7x, 128 devices: a whole 4x4x4 slice. The times are simulated.
128 devices in a mesh: rep: 8 (over z_lo, x), tp: 16 (over y, z_hi, core).
Axes of the slice: x: 4, y: 4, z: 4 (z_hi: 2, z_lo: 2; z = z_hi * 2 + z_lo), core: 2. Of those that a mesh axis runs over, the one named last changes fastest.
Arguments:
- batch_rows: bfloat16 [12288, 4096], P(('rep', 'tp')), may hold values from -6 to 6
- token_slots: int32 [8, 384], P('rep'), may hold values from 0 to 1535, as said below
- holder_map: int32 [8, 16], P('rep'), may hold values from -2 to 111, as said below
- copies: bfloat16 [32768, 16384], P('rep', 'tp'), may hold values from -6 to 6
- upstream: bfloat16 [3072, 16384], P('rep', 'tp'), may hold values from -18 to 18
- up_act: bfloat16 [3072, 16384], P('rep', 'tp'), may hold values from -6 to 6
- master: float32 [4096, 14336], P('rep', 'tp'), may hold values from -0.078125 to 0.078125
- moment1: bfloat16 [4096, 14336], P('rep', 'tp'), may hold values from -0.75 to 0.75
- moment2: bfloat16 [4096, 14336], P('rep', 'tp'), may hold values from 0.049804688 to 2
Outputs:
- master_next: float32 [4096, 14336], P('rep', 'tp')
- moment1_next: bfloat16 [4096, 14336], P('rep', 'tp')
- moment2_next: bfloat16 [4096, 14336], P('rep', 'tp')
- copy_next: bfloat16 [32768, 16384], P('rep', 'tp')
Inputs may be any that keep to these rules, and one draw needn't show every extreme that they name: `token_slots`: row r lists 384 distinct rows of replica r's batch. `holder_map`: each row is one replica. A row is either -1 everywhere, or holds -2 at exactly 2 devices and at every other device a distinct piece 7 * j + s (0 <= s < 7) with j one of that row's -2 devices, each such piece exactly once. 4 rows are of the second kind. Columns of copies, upstream and up_act that the steps do not name are not read.
All inputs are finite; a program needn't handle non-finite values.
Results may differ from a plain program's by a relative error of at most 0.02.
Values may be sent and summed in bfloat16 or wider, within the bound.
A program may use at most 128 MiB of HBM per device.

v0:
```python
import math
import jax
import jax.numpy as jnp
from jax import lax
from jax.sharding import PartitionSpec as P

beta_one = 0.9
beta_two = 0.95
bias_one = 1.0 - 0.9**10
bias_two = 1.0 - 0.95**10
learn_rate = 0.05
weight_decay = 0.1
epsilon = 1e-08


def from_everyone(array, axis):
    copies = jnp.broadcast_to(array, (lax.axis_size(axis), *array.shape))
    return lax.all_to_all(copies, axis, split_axis=0, concat_axis=0, tiled=True)


def joined_along(pieces, dim):
    shape = list(pieces.shape[1:])
    shape[dim] *= pieces.shape[0]
    return jnp.moveaxis(pieces, 0, dim).reshape(shape)


def gathered_copies(array, axis, dim):
    pieces = from_everyone(array, axis)
    return joined_along(pieces, dim)


def rows_for(lines, count):
    spare = -lines.shape[0] % count
    if not spare:
        return lines
    return jnp.concatenate([lines, jnp.zeros((spare, *lines.shape[1:]), lines.dtype)])


def sum_in_two_steps(array, axis):
    lines = array.reshape(-1, *array.shape[1:][-1:])
    own = lax.psum_scatter(
        rows_for(lines, lax.axis_size(axis)), axis, scatter_dimension=0, tiled=True
    )
    whole = lax.all_gather(own, axis).reshape(-1, *lines.shape[1:])
    return lax.slice_in_dim(whole, 0, len(lines)).reshape(array.shape)


def on_device(
    batch_rows, token_slots, holder_map, copies, upstream, up_act, master, moment1, moment2
):
    tp_count = lax.axis_size("tp")
    position = lax.axis_index("tp")
    chosen = token_slots[0]
    whole_batch = lax.all_gather(batch_rows, "tp", axis=0, tiled=True)
    inputs = jnp.take(whole_batch, chosen, axis=0)
    holders = holder_map[0]
    own_entry = jnp.take(holders, position)
    narrow = copies.shape[1]
    unit_cols = narrow // 8
    wide_cols = 7 * unit_cols
    scaling = 1.0 / math.sqrt(copies.shape[0])
    gate_pre = jnp.dot(inputs, copies, preferred_element_type=jnp.float32) * scaling
    logistic = jax.nn.sigmoid(gate_pre)
    gate_grad = (
        upstream.astype(jnp.float32)
        * up_act.astype(jnp.float32)
        * logistic
        * (1.0 + gate_pre * (1.0 - logistic))
    ).astype(jnp.bfloat16)
    tokens = gate_grad.shape[0]
    pooled = gathered_copies(gate_grad[:, wide_cols:], "tp", 1)
    pooled = pooled.reshape(tokens, tp_count, unit_cols)
    wanted = position * 7 + jnp.arange(7, dtype=jnp.int32)
    owners = jnp.argmax(holders[None, :] == wanted[:, None], axis=1)
    rebuilt = jnp.take(pooled, owners, axis=1).reshape(tokens, wide_cols)
    block_grad = jnp.where(own_entry == -2, rebuilt, gate_grad[:, :wide_cols])
    product = lax.dot_general(
        inputs, block_grad, (((0,), (0,)), ((), ())), preferred_element_type=jnp.float32
    )
    gradient = lax.psum_scatter(
        (product * scaling).astype(jnp.bfloat16), "rep", scatter_dimension=0, tiled=True
    ).astype(jnp.float32)
    first_new = beta_one * moment1.astype(jnp.float32) + (1.0 - beta_one) * gradient
    second_new = beta_two * moment2.astype(jnp.float32) + (1.0 - beta_two) * gradient * gradient
    step_size = first_new / bias_one / (jnp.sqrt(second_new / bias_two) + epsilon)
    master_next = master - learn_rate * (step_size + weight_decay * master)
    fresh_copy = master_next.astype(jnp.bfloat16)
    full_block = lax.all_gather(fresh_copy, "rep", axis=0, tiled=True)
    height = full_block.shape[0]
    failed_count = tp_count // 8
    root_list = jnp.nonzero(holders == -2, size=failed_count, fill_value=0)[0].astype(jnp.int32)
    slot_start = jnp.maximum(own_entry, 0) % 7 * unit_cols
    slot_ids = jnp.arange(failed_count, dtype=jnp.int32)
    my_slot = jnp.argmax(root_list == position)
    placing = (own_entry == -2) & (slot_ids == my_slot)
    placed = jnp.where(
        placing[None, :, None],
        full_block.astype(jnp.float32)[:, None, :],
        jnp.zeros((height, failed_count, wide_cols), jnp.float32),
    )
    summed = sum_in_two_steps(
        placed.reshape(height, failed_count * wide_cols).astype(jnp.bfloat16), "tp"
    ).astype(jnp.float32)
    summed = summed.astype(jnp.bfloat16)
    source_slot = jnp.argmax(root_list == jnp.maximum(own_entry, 0) // 7)
    adopted = lax.dynamic_slice_in_dim(summed, source_slot * wide_cols + slot_start, unit_cols, 1)
    adopted = jnp.where(own_entry >= 0, adopted, jnp.zeros_like(adopted))
    copy_next = jnp.concatenate([full_block, adopted], axis=1)
    copy_next = jnp.where(own_entry == -2, jnp.zeros_like(copy_next), copy_next)
    return (master_next, first_new.astype(jnp.bfloat16), second_new.astype(jnp.bfloat16), copy_next)


def solution(mesh):
    placed = (
        P(("rep", "tp"), None),
        P("rep", None),
        P("rep", None),
        P("rep", "tp"),
        P("rep", "tp"),
        P("rep", "tp"),
        P("rep", "tp"),
        P("rep", "tp"),
        P("rep", "tp"),
    )
    return jax.shard_map(
        on_device,
        mesh=mesh,
        in_specs=placed,
        out_specs=(P("rep", "tp"), P("rep", "tp"), P("rep", "tp"), P("rep", "tp")),
        check_vma=False,
    )
```

profile of v0, /device:TPU:1, one launch (start us, length us, event | category | flops | bytes accessed | tf_op | source)
XLA Modules:
  0.0 611.0 jit_solution(9419785542743542625)
XLA Ops:
  7.9 0.7 reduce.47
  8.6 0.7 fusion.9
  9.3 95.7 %all-gather.5.cloned.1.call-done = bf16[1536,4096]{1,0:T(8,128)(2,1)} async-done(((bf16[96,4096]{1,0:T(8,128)(2,1)}), bf16[1536,4096]{1,0:T(8,128)(2,1)}) %all-gather.5.cloned.1.call-update) | async-done | bytes 12582928 | tf_op jit(solution)/shard_map/all_gather | solution.py:54
  105.1 13.7 %gather_fusion = bf16[384,4096]{1,0:T(8,128)(2,1)S(1)} fusion(bf16[1536,4096]{1,0:T(8,128)(2,1)} %all-gather.5.cloned.1.call-done, s32[1024]{0:T(1024)S(1)} %pad_clamp_fusion.1), kind=kCustom, calls=%fused_computation | custom fusion | bytes 6292992 | tf_op jit(solution)/shard_map/jit(_take)/gather | solution.py:55
  118.8 8.9 %multiply_convert_fusion.1 = bf16[384,1024]{1,0:T(8,128)(2,1)S(1)} fusion(bf16[384,1024]{1,0:T(8,128)(2,1)} %param.14, bf16[384,1024]{1,0:T(8,128)(2,1)} %param.13, bf16[4096,1024]{1,0:T(8,128)(2,1)} %param.12, bf16[384,4096]{1,0:T(8,128)(2,1)S(1)} %gather_fusion, pred[384]{0:T(512)(128)(4,1)S(1)} %compare_and_fusion.2), kind=kOutput, calls=%fused_computation.12 | convolution fusion | flops 3227910144 | bytes 13894016 | tf_op jit(solution)/shard_map/dot_general | solution.py:62
  127.7 0.8 copy-done.3
  128.5 1.4 broadcast_in_dim.83
  130.0 3.9 all-to-all-start
  135.4 0.7 iota_reduce_fusion
  136.2 20.6 %all-to-all-done = bf16[16,384,128]{2,1,0:T(8,128)(2,1)S(1)} async-done(((bf16[16,384,128]{2,1,0:T(8,128)(2,1)}), bf16[16,384,128]{2,1,0:T(8,128)(2,1)S(1)}, u32[]{:S(2)}, u32[]{:S(2)}) %all-to-all-start) | async-done | bytes 1572896 | tf_op jit(solution)/shard_map/all_to_all | solution.py:18
  158.2 8.6 %multiply_convert_fusion = bf16[4096,896]{1,0:T(8,128)(2,1)} fusion(bf16[384,4096]{1,0:T(8,128)(2,1)} %copy-done, pred[384]{0:T(512)(128)(4,1)S(1)} %compare_and_fusion.2, bf16[384,1024]{1,0:T(8,128)(2,1)S(1)} %copy-done.4, bf16[384,896]{1,0:T(8,128)(2,1)S(1)} %copy.18, pred[896]{0:T(1024)(128)(4,1)S(1)} %broadcast_bitcast_fusion, pred[]{:T(512)} %bitcast.3), kind=kOutput, calls=%fused_computation.4 | convolution fusion | flops 2828173312 | bytes 11863553 | tf_op jit(solution)/shard_map/dot_general | solution.py:77
  166.9 81.4 %reduce-scatter.3.cloned.1.call-done = bf16[512,896]{1,0:T(8,128)(2,1)} async-done(((bf16[4096,896]{1,0:T(8,128)(2,1)}), bf16[512,896]{1,0:T(8,128)(2,1)}) %reduce-scatter.3.cloned.1.call-update) | async-done | bytes 917520 | tf_op jit(solution)/shard_map/reduce_scatter | solution.py:80
  248.3 5.7 fusion.17
  255.2 0.7 fusion.10
  255.9 1.4 compare_reduce_fusion.1
  258.0 77.0 %all-gather.7.cloned.1.call-done = bf16[4096,896]{1,0:T(8,128)(2,1)} async-done(((bf16[512,896]{1,0:T(8,128)(2,1)}), bf16[4096,896]{1,0:T(8,128)(2,1)}) %all-gather.7.cloned.1.call-update) | async-done | bytes 7340048 | tf_op jit(solution)/shard_map/all_gather | solution.py:88
  335.0 10.4 %broadcast_in_dim.91 = bf16[4096,2,896]{2,1,0:T(2,128)(2,1)} broadcast(bf16[4096,896]{1,0:T(8,128)(2,1)} %all-gather.7.cloned.1.call-done), dimensions={0,2} | broadcast | bytes 22020096 | tf_op jit(solution)/shard_map/jit(_where)/broadcast_in_dim | solution.py:96
  345.4 10.0 %copy.20 = bf16[512,8,2,896]{3,1,2,0:T(8,128)(2,1)S(1)} copy(bf16[512,8,2,896]{3,2,1,0:T(2,128)(2,1)} %bitcast.29) | data formatting | bytes 29360128
  355.5 7.2 %select_convert_fusion = bf16[4096,1792]{1,0:T(8,128)(2,1)} fusion(bf16[4096,1792]{1,0:T(8,128)(2,1)S(1)} %bitcast.28, pred[1792]{0:T(1024)(128)(4,1)S(1)} %broadcast_in_dim.89), kind=kLoop, calls=%fused_computation.3 | loop fusion | flops 7340032 | bytes 29361920 | tf_op jit(solution)/shard_map/convert_element_type | solution.py:102
  362.8 130.8 %reduce-scatter.5.cloned.1.call-done = bf16[256,1792]{1,0:T(8,128)(2,1)} async-done(((bf16[4096,1792]{1,0:T(8,128)(2,1)}), bf16[256,1792]{1,0:T(8,128)(2,1)}) %reduce-scatter.5.cloned.1.call-update) | async-done | bytes 917520 | tf_op jit(solution)/shard_map/reduce_scatter | solution.py:41
  493.6 1.3 compare_reduce_fusion
  495.5 100.2 %all-gather.9.cloned.1.call-done = bf16[4096,1792]{1,0:T(8,128)(2,1)} async-done(((bf16[256,1792]{1,0:T(8,128)(2,1)}), bf16[4096,1792]{1,0:T(8,128)(2,1)}) %all-gather.9.cloned.1.call-update) | async-done | bytes 14680080 | tf_op jit(solution)/shard_map/all_gather | solution.py:44
  595.7 1.4 dynamic-slice_select_fusion
  597.1 7.3 %maximum_select_fusion = bf16[4096,1024]{1,0:T(8,128)(2,1)} fusion(bf16[4096,128]{1,0:T(8,128)(2,1)S(1)} %dynamic-slice_select_fusion, bf16[4096,896]{1,0:T(8,128)(2,1)} %all-gather.7.cloned.1.call-done, pred[]{:T(512)} %bitcast.3), kind=kLoop, calls=%fused_computation.5 | loop fusion | flops 20971520 | bytes 16777216 | tf_op jit(solution)/shard_map/jit(_where)/select_n | solution.py:109
  (43 shorter events, 5.1 us)
Async XLA Ops:
  7.2 97.9 %all-gather.5.cloned.1.call-start = ((), (), s32[]{:S(2)}) async-start(), calls=%async_computation.3 | async-start | bytes 13369344 | tf_op jit(solution)/shard_map/all_gather | solution.py:54
  118.8 8.9 %copy-start = (bf16[384,4096]{1,0:T(8,128)(2,1)}, bf16[384,4096]{1,0:T(8,128)(2,1)S(1)}, u32[]{:S(2)}) copy-start(bf16[384,4096]{1,0:T(8,128)(2,1)S(1)} %gather_fusion) | copy-start | bytes 9437188
  127.7 0.9 copy-start.3
  130.0 4.1 copy-start.5
  130.0 26.8 %all-to-all-start = ((bf16[16,384,128]{2,1,0:T(8,128)(2,1)}), bf16[16,384,128]{2,1,0:T(8,128)(2,1)S(1)}, u32[]{:S(2)}, u32[]{:S(2)}) async-start(bf16[16,384,128]{2,1,0:T(8,128)(2,1)} %broadcast_in_dim.83), calls=%async_computation | async-start | bytes 3145728 | tf_op jit(solution)/shard_map/all_to_all | solution.py:18
  133.9 114.4 %reduce-scatter.3.cloned.1.call-start = ((), (), s32[]{:S(2)}) async-start(), calls=%async_computation.4 | async-start | bytes 8257536 | tf_op jit(solution)/shard_map/reduce_scatter | solution.py:80
  156.8 1.4 copy-start.4
  166.8 81.5 %copy-start.1 = (f32[512,896]{1,0:T(8,128)S(1)}, f32[512,896]{1,0:T(8,128)}, u32[]{:S(2)}) copy-start(f32[512,896]{1,0:T(8,128)} %param.15) | copy-start | bytes 5505028
  166.8 81.5 %copy-start.2 = (bf16[512,896]{1,0:T(8,128)(2,1)S(1)}, bf16[512,896]{1,0:T(8,128)(2,1)}, u32[]{:S(2)}) copy-start(bf16[512,896]{1,0:T(8,128)(2,1)} %param.17) | copy-start | bytes 2752516
  166.8 168.2 %all-gather.7.cloned.1.call-start = ((), (), s32[]{:S(2)}) async-start(), calls=%async_computation.5 | async-start | bytes 8257536 | tf_op jit(solution)/shard_map/all_gather | solution.py:88
  254.0 239.5 %reduce-scatter.5.cloned.1.call-start = ((), (), s32[]{:S(2)}) async-start(), calls=%async_computation.6 | async-start | bytes 15597568 | tf_op jit(solution)/shard_map/reduce_scatter | solution.py:41
  362.7 233.0 %all-gather.9.cloned.1.call-start = ((), (), s32[]{:S(2)}) async-start(), calls=%async_computation.7 | async-start | bytes 15597568 | tf_op jit(solution)/shard_map/all_gather | solution.py:44
Sparse Core Ops, SparseCore 0:
  10.4 94.6 all-gather.4
  166.9 81.2 reduce-scatter.2
  254.2 80.8 all-gather.6
  362.9 130.6 reduce-scatter.4
  496.1 99.5 all-gather.8
where the time goes:
time: 612 us; the launch traced here: 611 us
  waiting for transfers between devices  506 us (83%)
  local copies, waits for them, and re-layouts  38.7 us (6%)
  other arithmetic  29 us (5%)
  matrix products  17.5 us (3%)
  between operations  15.2 us (2%)
    reduce_scatter x1, waiting for transfers between devices, sum_in_two_steps(): lax.psum_scatter(rows_for(lines, lax.axis_size(axis)), axis, scatter_dime...  131 us
    all_gather x1, waiting for transfers between devices, sum_in_two_steps(): whole = lax.all_gather(own, axis).reshape(-1, *lines.shape[1:])  100 us
    all_gather x1, waiting for transfers between devices, on_device(): whole_batch = lax.all_gather(batch_rows, 'tp', axis=0, tiled=True)  95.7 us
    reduce_scatter x1, waiting for transfers between devices, on_device(): lax.psum_scatter((product * scaling).astype(jnp.bfloat16), 'rep', scatter...  81.4 us
    all_gather x1, waiting for transfers between devices, on_device(): full_block = lax.all_gather(fresh_copy, 'rep', axis=0, tiled=True)  77 us
    all_to_all x1, waiting for transfers between devices, from_everyone(): return lax.all_to_all(copies, axis, split_axis=0, concat_axis=0, tiled=True)  20.6 us
    gather x1, local copies, waits for them, and re-layouts, on_device(): inputs = jnp.take(whole_batch, chosen, axis=0)  13.7 us
  transfers between devices with their start and end apart: 6, of which 6 were waited for; matrix products, arithmetic and copies ran while one was open for 1% of the time, Pallas kernels for 0%

commit v1 on v0

--- a/solution.py
+++ b/solution.py
@@ -51,7 +51,9 @@
     tp_count = lax.axis_size("tp")
     position = lax.axis_index("tp")
     chosen = token_slots[0]
-    whole_batch = lax.all_gather(batch_rows, "tp", axis=0, tiled=True)
+    whole_batch = jnp.concatenate(
+        lax.all_to_all(jnp.stack([batch_rows] * lax.axis_size("tp")), "tp", 0, 0), axis=0
+    )
     inputs = jnp.take(whole_batch, chosen, axis=0)
     holders = holder_map[0]
     own_entry = jnp.take(holders, position)

time: 612 us -> 735 us (1.20)
  waiting for transfers between devices: 506 us -> 610 us
  starting transfers between devices: 4.26 us -> 18.1 us
    all_to_all x0 -> x1, waiting for transfers between devices: none -> 200 us  [on_device(): lax.all_to_all(jnp.stack([batch_rows] * lax.axis_size('tp')), 'tp', 0, 0)]
    all_gather x1 -> x0, waiting for transfers between devices: 95.7 us -> none  [on_device(): whole_batch = lax.all_gather(batch_rows, 'tp', axis=0, tiled=True)]
    all_to_all x0 -> x1, starting transfers between devices: none -> 9.43 us  [on_device(): lax.all_to_all(jnp.stack([batch_rows] * lax.axis_size('tp')), 'tp', 0, 0)]
where the time goes in v1:
time: 735 us
  waiting for transfers between devices  610 us (83%)
  local copies, waits for them, and re-layouts  45.9 us (6%)
  other arithmetic  27.6 us (4%)
  starting transfers between devices  18.1 us (2%)
  matrix products  17.5 us (2%)
  between operations  15.2 us (2%)
    all_to_all x1, waiting for transfers between devices, on_device(): lax.all_to_all(jnp.stack([batch_rows] * lax.axis_size('tp')), 'tp', 0, 0)  200 us
    reduce_scatter x1, waiting for transfers between devices, sum_in_two_steps(): lax.psum_scatter(rows_for(lines, lax.axis_size(axis)), axis, scatter_dime...  131 us
    all_gather x1, waiting for transfers between devices, sum_in_two_steps(): whole = lax.all_gather(own, axis).reshape(-1, *lines.shape[1:])  100 us
    reduce_scatter x1, waiting for transfers between devices, on_device(): lax.psum_scatter((product * scaling).astype(jnp.bfloat16), 'rep', scatter...  81.7 us
    all_gather x1, waiting for transfers between devices, on_device(): full_block = lax.all_gather(fresh_copy, 'rep', axis=0, tiled=True)  76.9 us
    all_to_all x1, waiting for transfers between devices, from_everyone(): return lax.all_to_all(copies, axis, split_axis=0, concat_axis=0, tiled=True)  20.5 us
  transfers between devices with their start and end apart: 6, of which 6 were waited for; matrix products, arithmetic and copies ran while one was open for 1% of the time, Pallas kernels for 0%

profile of v1, /device:TPU:1, one launch (start us, length us, event | category | flops | bytes accessed | tf_op | source)
XLA Modules:
  0.0 734.6 jit_solution(12424222608031279006)
XLA Ops:
  7.2 7.2 stack.2
  14.4 9.4 %all-to-all-start = ((bf16[16,96,4096]{2,1,0:T(8,128)(2,1)}), bf16[16,96,4096]{2,1,0:T(8,128)(2,1)}, u32[]{:S(2)}, u32[]{:S(2)}) async-start(bf16[16,96,4096]{2,1,0:T(8,128)(2,1)} %stack.2), calls=%async_computation | async-start | bytes 25165824 | tf_op jit(solution)/shard_map/all_to_all | solution.py:55
  23.9 200.1 %all-to-all-done = bf16[16,96,4096]{2,1,0:T(8,128)(2,1)} async-done(((bf16[16,96,4096]{2,1,0:T(8,128)(2,1)}), bf16[16,96,4096]{2,1,0:T(8,128)(2,1)}, u32[]{:S(2)}, u32[]{:S(2)}) %all-to-all-start) | async-done | bytes 12582944 | tf_op jit(solution)/shard_map/all_to_all | solution.py:55
  224.0 13.7 %gather_fusion = bf16[384,4096]{1,0:T(8,128)(2,1)S(1)} fusion(bf16[1536,4096]{1,0:T(8,128)(2,1)} %bitcast, s32[1024]{0:T(1024)S(1)} %pad_clamp_fusion.1), kind=kCustom, calls=%fused_computation | custom fusion | bytes 6292992 | tf_op jit(solution)/shard_map/jit(_take)/gather | solution.py:57
  237.7 8.9 %multiply_convert_fusion.1 = bf16[384,1024]{1,0:T(8,128)(2,1)S(1)} fusion(bf16[384,1024]{1,0:T(8,128)(2,1)} %param.14, bf16[384,1024]{1,0:T(8,128)(2,1)} %param.13, bf16[4096,1024]{1,0:T(8,128)(2,1)} %param.12, bf16[384,4096]{1,0:T(8,128)(2,1)S(1)} %gather_fusion, pred[384]{0:T(512)(128)(4,1)S(1)} %compare_and_fusion.2), kind=kOutput, calls=%fused_computation.12 | convolution fusion | flops 3227910144 | bytes 13894016 | tf_op jit(solution)/shard_map/dot_general | solution.py:64
  246.6 0.8 copy-done.3
  247.5 1.4 broadcast_in_dim.83
  248.9 8.3 %all-to-all-start.1 = ((bf16[16,384,128]{2,1,0:T(8,128)(2,1)}), bf16[16,384,128]{2,1,0:T(8,128)(2,1)S(1)}, u32[]{:S(2)}, u32[]{:S(2)}) async-start(bf16[16,384,128]{2,1,0:T(8,128)(2,1)} %broadcast_in_dim.83), calls=%async_computation.1 | async-start | bytes 3145728 | tf_op jit(solution)/shard_map/all_to_all | solution.py:18
  258.7 0.7 iota_reduce_fusion
  259.5 20.5 %all-to-all-done.1 = bf16[16,384,128]{2,1,0:T(8,128)(2,1)S(1)} async-done(((bf16[16,384,128]{2,1,0:T(8,128)(2,1)}), bf16[16,384,128]{2,1,0:T(8,128)(2,1)S(1)}, u32[]{:S(2)}, u32[]{:S(2)}) %all-to-all-start.1) | async-done | bytes 1572896 | tf_op jit(solution)/shard_map/all_to_all | solution.py:18
  281.5 8.6 %multiply_convert_fusion = bf16[4096,896]{1,0:T(8,128)(2,1)} fusion(bf16[384,4096]{1,0:T(8,128)(2,1)} %copy-done, pred[384]{0:T(512)(128)(4,1)S(1)} %compare_and_fusion.2, bf16[384,1024]{1,0:T(8,128)(2,1)S(1)} %copy-done.4, bf16[384,896]{1,0:T(8,128)(2,1)S(1)} %copy.18, pred[896]{0:T(1024)(128)(4,1)S(1)} %broadcast_bitcast_fusion, pred[]{:T(512)} %bitcast.4), kind=kOutput, calls=%fused_computation.4 | convolution fusion | flops 2828173312 | bytes 11863553 | tf_op jit(solution)/shard_map/dot_general | solution.py:79
  290.1 81.7 %reduce-scatter.3.cloned.1.call-done = bf16[512,896]{1,0:T(8,128)(2,1)} async-done(((bf16[4096,896]{1,0:T(8,128)(2,1)}), bf16[512,896]{1,0:T(8,128)(2,1)}) %reduce-scatter.3.cloned.1.call-update) | async-done | bytes 917520 | tf_op jit(solution)/shard_map/reduce_scatter | solution.py:82
  371.9 5.7 fusion.17
  378.8 0.7 fusion.10
  379.5 1.4 compare_reduce_fusion.1
  381.6 76.9 %all-gather.4.cloned.1.call-done = bf16[4096,896]{1,0:T(8,128)(2,1)} async-done(((bf16[512,896]{1,0:T(8,128)(2,1)}), bf16[4096,896]{1,0:T(8,128)(2,1)}) %all-gather.4.cloned.1.call-update) | async-done | bytes 7340048 | tf_op jit(solution)/shard_map/all_gather | solution.py:90
  458.6 10.4 %broadcast_in_dim.91 = bf16[4096,2,896]{2,1,0:T(2,128)(2,1)} broadcast(bf16[4096,896]{1,0:T(8,128)(2,1)} %all-gather.4.cloned.1.call-done), dimensions={0,2} | broadcast | bytes 22020096 | tf_op jit(solution)/shard_map/jit(_where)/broadcast_in_dim | solution.py:98
  469.0 10.0 %copy.20 = bf16[512,8,2,896]{3,1,2,0:T(8,128)(2,1)S(1)} copy(bf16[512,8,2,896]{3,2,1,0:T(2,128)(2,1)} %bitcast.30) | data formatting | bytes 29360128
  479.0 7.2 select_convert_fusion
  486.3 130.8 %reduce-scatter.5.cloned.1.call-done = bf16[256,1792]{1,0:T(8,128)(2,1)} async-done(((bf16[4096,1792]{1,0:T(8,128)(2,1)}), bf16[256,1792]{1,0:T(8,128)(2,1)}) %reduce-scatter.5.cloned.1.call-update) | async-done | bytes 917520 | tf_op jit(solution)/shard_map/reduce_scatter | solution.py:41
  617.2 1.3 compare_reduce_fusion
  619.1 100.2 %all-gather.6.cloned.1.call-done = bf16[4096,1792]{1,0:T(8,128)(2,1)} async-done(((bf16[256,1792]{1,0:T(8,128)(2,1)}), bf16[4096,1792]{1,0:T(8,128)(2,1)}) %all-gather.6.cloned.1.call-update) | async-done | bytes 14680080 | tf_op jit(solution)/shard_map/all_gather | solution.py:44
  719.2 1.4 dynamic-slice_select_fusion
  720.7 7.3 maximum_select_fusion
  (45 shorter events, 4.4 us)
Async XLA Ops:
  14.4 9.4 %copy-start.5 = (s32[1,384]{1,0:T(1,128)S(1)}, s32[1,384]{1,0:T(1,128)}, u32[]{:S(2)}) copy-start(s32[1,384]{1,0:T(1,128)} %param.10) | copy-start | bytes 4612
  14.4 209.6 %all-to-all-start = ((bf16[16,96,4096]{2,1,0:T(8,128)(2,1)}), bf16[16,96,4096]{2,1,0:T(8,128)(2,1)}, u32[]{:S(2)}, u32[]{:S(2)}) async-start(bf16[16,96,4096]{2,1,0:T(8,128)(2,1)} %stack.2), calls=%async_computation | async-start | bytes 25165824 | tf_op jit(solution)/shard_map/all_to_all | solution.py:55
  237.7 8.9 %copy-start = (bf16[384,4096]{1,0:T(8,128)(2,1)}, bf16[384,4096]{1,0:T(8,128)(2,1)S(1)}, u32[]{:S(2)}) copy-start(bf16[384,4096]{1,0:T(8,128)(2,1)S(1)} %gather_fusion) | copy-start | bytes 9437188
  246.6 0.9 copy-start.3
  248.9 8.6 %copy-start.6 = (s32[1,16]{1,0:T(1,128)S(1)}, s32[1,16]{1,0:T(1,128)}, u32[]{:S(2)}) copy-start(s32[1,16]{1,0:T(1,128)} %param.11) | copy-start | bytes 196
  248.9 31.1 %all-to-all-start.1 = ((bf16[16,384,128]{2,1,0:T(8,128)(2,1)}), bf16[16,384,128]{2,1,0:T(8,128)(2,1)S(1)}, u32[]{:S(2)}, u32[]{:S(2)}) async-start(bf16[16,384,128]{2,1,0:T(8,128)(2,1)} %broadcast_in_dim.83), calls=%async_computation.1 | async-start | bytes 3145728 | tf_op jit(solution)/shard_map/all_to_all | solution.py:18
  257.2 114.6 %reduce-scatter.3.cloned.1.call-start = ((), (), s32[]{:S(2)}) async-start(), calls=%async_computation.4 | async-start | bytes 8257536 | tf_op jit(solution)/shard_map/reduce_scatter | solution.py:82
  280.1 1.4 copy-start.4
  290.1 81.8 %copy-start.1 = (f32[512,896]{1,0:T(8,128)S(1)}, f32[512,896]{1,0:T(8,128)}, u32[]{:S(2)}) copy-start(f32[512,896]{1,0:T(8,128)} %param.15) | copy-start | bytes 5505028
  290.1 81.8 %copy-start.2 = (bf16[512,896]{1,0:T(8,128)(2,1)S(1)}, bf16[512,896]{1,0:T(8,128)(2,1)}, u32[]{:S(2)}) copy-start(bf16[512,896]{1,0:T(8,128)(2,1)} %param.17) | copy-start | bytes 2752516
  290.1 168.5 %all-gather.4.cloned.1.call-start = ((), (), s32[]{:S(2)}) async-start(), calls=%async_computation.5 | async-start | bytes 8257536 | tf_op jit(solution)/shard_map/all_gather | solution.py:90
  377.6 239.5 %reduce-scatter.5.cloned.1.call-start = ((), (), s32[]{:S(2)}) async-start(), calls=%async_computation.6 | async-start | bytes 15597568 | tf_op jit(solution)/shard_map/reduce_scatter | solution.py:41
  486.3 233.0 %all-gather.6.cloned.1.call-start = ((), (), s32[]{:S(2)}) async-start(), calls=%async_computation.7 | async-start | bytes 15597568 | tf_op jit(solution)/shard_map/all_gather | solution.py:44
Sparse Core Ops, SparseCore 0:
  290.2 81.5 reduce-scatter.2
  377.7 80.7 all-gather.3
  486.4 130.6 reduce-scatter.4
  619.7 99.5 all-gather.5
